TPU v7x, 32 devices: a whole 2x2x4 slice. The times are simulated.
32 devices in a mesh: dp: 8 (over z, y), tensor: 4 (over x, core).
Axes of the slice: x: 2, y: 2, z: 4, core: 2. Of those that a mesh axis runs over, the one named last changes fastest.
Arguments:
- tokens: bfloat16 [8192, 1536], P('dp', 'tensor'), may hold values from -6 to 6
- segments: int32 [8, 1024], P('dp'), may hold values from 0 to 7, never falling along the last dimension, each value on 1 to 512 neighbouring positions
- attn_gain: bfloat16 [1536], P('tensor'), may hold values from 0.25 to 1.75
- w_qkv: bfloat16 [3, 1536, 1536], P(None, None, 'tensor'), may hold values from -0.15625 to 0.15625
- kq_kernel: float32 [16, 6, 11], P('tensor'), may hold values from -0.8 to 1.8
- head_mix: float32 [16, 2], P('tensor'), may hold values from -0.6 to 1.3
- group_gain: bfloat16 [1536], P('tensor'), may hold values from 0.25 to 1.75
- w_out: bfloat16 [1536, 1536], P('tensor'), may hold values from -0.15625 to 0.15625
- mlp_gain: bfloat16 [1536], P('tensor'), may hold values from 0.25 to 1.75
- w_gate_up: bfloat16 [2, 1536, 4096], P(None, None, 'tensor'), may hold values from -0.15625 to 0.15625
- w_down: bfloat16 [4096, 1536], P('tensor'), may hold values from -0.09375 to 0.09375
- cotangent: bfloat16 [8192, 1536], P('dp', 'tensor'), may hold values from -6 to 6
Outputs:
- layer_out: bfloat16 [8192, 1536], P('dp', 'tensor')
- tokens_grad: float32 [8192, 1536], P('dp', 'tensor')
- attn_gain_grad: float32 [1536], P('tensor')
- w_qkv_grad: float32 [3, 1536, 1536], P(None, None, 'tensor')
- kq_kernel_grad: float32 [16, 6, 11], P('tensor')
- head_mix_grad: float32 [16, 2], P('tensor')
- group_gain_grad: float32 [1536], P('tensor')
- w_out_grad: float32 [1536, 1536], P('tensor')
- mlp_gain_grad: float32 [1536], P('tensor')
- w_gate_up_grad: float32 [2, 1536, 4096], P(None, None, 'tensor')
- w_down_grad: float32 [4096, 1536], P('tensor')
Inputs may be any that keep to these rules, and one draw needn't show every extreme that they name: `segments`: within a sequence the numbers never fall; each document holds at most 512 tokens.
All inputs are finite; a program needn't handle non-finite values.
Results may differ from a plain program's by a relative error of at most 0.018.
The roundings to bfloat16 on the way count: a program that leaves them out, or rounds other values in their place, can miss the bound.
Values may be sent and summed in bfloat16 or wider, within the bound.
A program may use at most 320 MiB of HBM per device.

v0:
```python
import jax
import jax.numpy as jnp
from jax import lax
from jax.sharding import PartitionSpec as P

HEAD_DIM = 96
EPS = 1e-05
NEG = -1e30
HIGH = lax.Precision.HIGHEST


def valid_pairs(seg_row):
    length = seg_row.shape[0]
    place = lax.iota(jnp.int32, length)
    return (place[None, :] <= place[:, None]) & (seg_row[:, None] == seg_row[None, :])


def padded_scores(masked, kernel):
    query_taps = kernel.shape[1]
    key_half = kernel.shape[2] // 2
    return jnp.pad(masked, ((0, 0), (query_taps - 1, 0), (key_half, key_half)))


def conv_window(padded, kernel, query_shift, key_shift, length):
    query_taps = kernel.shape[1]
    key_taps = kernel.shape[2]
    row_start = query_taps - 1 - query_shift
    col_start = key_taps - 1 - key_shift
    return lax.slice(
        padded, (0, row_start, col_start), (padded.shape[0], row_start + length, col_start + length)
    )


def kq_conv(masked, kernel):
    length = masked.shape[1]
    padded = padded_scores(masked, kernel)
    summed = jnp.zeros(masked.shape, jnp.float32)
    for query_shift in range(kernel.shape[1]):
        for key_shift in range(kernel.shape[2]):
            shifted = conv_window(padded, kernel, query_shift, key_shift, length)
            summed = summed + kernel[:, query_shift, key_shift][:, None, None] * shifted
    return summed


def conv_back(grad_logits, masked, kernel):
    query_taps = kernel.shape[1]
    key_taps = kernel.shape[2]
    key_half = key_taps // 2
    heads_here = masked.shape[0]
    length = masked.shape[1]
    padded_in = padded_scores(masked, kernel)
    padded_grad = jnp.pad(grad_logits, ((0, 0), (0, query_taps - 1), (key_half, key_half)))
    grad_masked = jnp.zeros(masked.shape, jnp.float32)
    kernel_terms = []
    for query_shift in range(query_taps):
        for key_shift in range(key_taps):
            window_in = conv_window(padded_in, kernel, query_shift, key_shift, length)
            window_grad = lax.slice(
                padded_grad,
                (0, query_shift, key_shift),
                (heads_here, query_shift + length, key_shift + length),
            )
            grad_masked = (
                grad_masked + kernel[:, query_shift, key_shift][:, None, None] * window_grad
            )
            kernel_terms.append(jnp.sum(grad_logits * window_in, axis=(1, 2)))
    grad_kernel = jnp.stack(kernel_terms, axis=1).reshape(heads_here, query_taps, key_taps)
    return (grad_masked, grad_kernel)


def mix_heads(probs, mix):
    heads_here = probs.shape[0]
    length = probs.shape[1]
    paired = probs.reshape(heads_here // 2, 2, length, length)
    weights = mix.reshape(heads_here // 2, 2, 2)
    first = weights[:, :, 0][:, :, None, None] * paired[:, 0][:, None]
    second = weights[:, :, 1][:, :, None, None] * paired[:, 1][:, None]
    return (first + second).reshape(heads_here, length, length)


def mix_back(grad_mixed, probs, mix):
    heads_here = probs.shape[0]
    length = probs.shape[1]
    paired_grad = grad_mixed.reshape(heads_here // 2, 2, length, length)
    paired = probs.reshape(heads_here // 2, 2, length, length)
    weights = mix.reshape(heads_here // 2, 2, 2)
    grad_probs = (
        weights[:, 0, :][:, :, None, None] * paired_grad[:, 0][:, None]
        + weights[:, 1, :][:, :, None, None] * paired_grad[:, 1][:, None]
    )
    grad_mix = jnp.einsum("grqk,gsqk->grs", paired_grad, paired, precision=HIGH)
    return (grad_probs.reshape(heads_here, length, length), grad_mix.reshape(heads_here, 2))


def score_logits(query, keys, seg_row, kernel):
    scale = query.shape[2] ** (-0.5)
    valid = valid_pairs(seg_row)[None]
    raw = jnp.einsum("qhd,khd->hqk", query, keys, preferred_element_type=jnp.float32)
    masked = jnp.where(valid, raw * scale, 0.0)
    logits = jnp.where(valid, kq_conv(masked, kernel), NEG)
    return (valid, masked, logits)


def attend_forward(query, keys, values, seg_row, kernel, mix):
    valid, masked, logits = score_logits(query, keys, seg_row, kernel)
    peak = jnp.max(logits, axis=-1, keepdims=True)
    expo = jnp.exp(logits - peak)
    summed = jnp.sum(expo, axis=-1, keepdims=True)
    probs = expo / summed
    mixed = mix_heads(probs, mix).astype(jnp.bfloat16)
    output = jnp.einsum("hqk,khd->qhd", mixed, values, preferred_element_type=jnp.float32)
    return (output, (peak + jnp.log(summed))[..., 0])


def attend_backward(query, keys, values, seg_row, grad_out, log_norm, kernel, mix):
    scale = query.shape[2] ** (-0.5)
    valid, masked, logits = score_logits(query, keys, seg_row, kernel)
    probs = jnp.exp(logits - log_norm[..., None])
    mixed = mix_heads(probs, mix).astype(jnp.bfloat16)
    grad_values = jnp.einsum("hqk,qhd->khd", mixed, grad_out, preferred_element_type=jnp.float32)
    grad_mixed = jnp.einsum("qhd,khd->hqk", grad_out, values, preferred_element_type=jnp.float32)
    grad_probs, grad_mix = mix_back(grad_mixed, probs, mix)
    grad_logits = probs * (grad_probs - jnp.sum(grad_probs * probs, axis=-1, keepdims=True))
    grad_masked, grad_kernel = conv_back(grad_logits, masked, kernel)
    grad_scores = (jnp.where(valid, grad_masked, 0.0) * scale).astype(jnp.bfloat16)
    grad_query = jnp.einsum("hqk,khd->qhd", grad_scores, keys, preferred_element_type=jnp.float32)
    grad_keys = jnp.einsum("hqk,qhd->khd", grad_scores, query, preferred_element_type=jnp.float32)
    return (grad_query, grad_keys, grad_values, grad_kernel, grad_mix)


def contract_rows(left, right):
    return lax.dot_general(
        left, right, (((0,), (0,)), ((), ())), preferred_element_type=jnp.float32
    )


def contract_cols(left, right):
    return lax.dot_general(
        left, right, (((1,), (1,)), ((), ())), preferred_element_type=jnp.float32
    )


def on_device(
    tokens,
    segments,
    attn_gain,
    w_qkv,
    kq_kernel,
    head_mix,
    group_gain,
    w_out,
    mlp_gain,
    w_gate_up,
    w_down,
    cotangent,
):
    rank = lax.axis_index("tensor")
    rows_here = tokens.shape[0]
    local_width = tokens.shape[1]
    seq_count = segments.shape[0]
    length = segments.shape[1]
    heads_here = w_qkv.shape[2] // HEAD_DIM
    start = rank * local_width
    gathered, gain_one, gain_two = (
        lax.all_gather(tokens, "tensor", axis=1, tiled=True),
        lax.all_gather(attn_gain, "tensor", axis=0, tiled=True),
        lax.all_gather(mlp_gain, "tensor", axis=0, tiled=True),
    )
    resid = gathered.astype(jnp.float32)
    full_width = resid.shape[1]
    scale_one = lax.rsqrt(jnp.mean(resid * resid, axis=-1, keepdims=True) + EPS)
    unit_one = resid * scale_one
    normed_one = (unit_one * gain_one.astype(jnp.float32)).astype(jnp.bfloat16)
    projected = jnp.einsum(
        "td,cde->cte", normed_one, w_qkv, preferred_element_type=jnp.float32
    ).astype(jnp.bfloat16)
    split_heads = projected.reshape(3, seq_count, length, heads_here, HEAD_DIM)

    def forward_one(items):
        return attend_forward(items[0], items[1], items[2], items[3], kq_kernel, head_mix)

    heads_out, log_norms = lax.map(
        forward_one, (split_heads[0], split_heads[1], split_heads[2], segments)
    )
    heads_out = heads_out.reshape(rows_here, heads_here, HEAD_DIM)
    group_scale = lax.rsqrt(jnp.mean(heads_out * heads_out, axis=-1, keepdims=True) + EPS)
    unit_heads = heads_out * group_scale
    gain_heads = group_gain.astype(jnp.float32).reshape(heads_here, HEAD_DIM)
    grouped = (unit_heads * gain_heads).astype(jnp.bfloat16).reshape(rows_here, local_width)
    attn_part = jnp.dot(grouped, w_out, preferred_element_type=jnp.float32)
    gain_full = gain_two.astype(jnp.float32)
    attn = lax.psum(attn_part, "tensor")
    hidden = resid + attn
    scale_two = lax.rsqrt(jnp.mean(hidden * hidden, axis=-1, keepdims=True) + EPS)
    unit_two = hidden * scale_two
    normed_two = (unit_two * gain_full).astype(jnp.bfloat16)
    hidden_local = lax.dynamic_slice_in_dim(hidden, start, local_width, 1)
    gate_up = jnp.einsum("td,cdf->ctf", normed_two, w_gate_up, preferred_element_type=jnp.float32)
    gate = gate_up[0]
    up = gate_up[1]
    sigmoid = jax.nn.sigmoid(gate)
    swish = gate * sigmoid
    act = (swish * up).astype(jnp.bfloat16)
    mlp_part = jnp.dot(act, w_down, preferred_element_type=jnp.float32)
    mlp_local = lax.psum_scatter(
        mlp_part.astype(jnp.bfloat16), "tensor", scatter_dimension=1, tiled=True
    ).astype(jnp.float32)
    layer_out = (hidden_local + mlp_local).astype(jnp.bfloat16)
    full_cot = lax.all_gather(cotangent, "tensor", axis=1, tiled=True)
    grad_down = contract_rows(act, full_cot)
    grad_act = contract_cols(full_cot, w_down)
    grad_gate = grad_act * up * sigmoid * (1.0 + gate * (1.0 - sigmoid))
    grad_up = grad_act * swish
    grad_pair = jnp.stack([grad_gate, grad_up]).astype(jnp.bfloat16)
    grad_gate_up = jnp.einsum(
        "td,ctf->cdf", normed_two, grad_pair, preferred_element_type=jnp.float32
    )
    grad_two_part = jnp.einsum(
        "ctf,cdf->td", grad_pair, w_gate_up, preferred_element_type=jnp.float32
    )
    grad_two = lax.psum(grad_two_part, "tensor")
    grad_gain_two = lax.dynamic_slice_in_dim(
        jnp.sum(grad_two * unit_two, axis=0), start, local_width, 0
    )
    scaled_two = grad_two * gain_full
    grad_hidden = full_cot.astype(jnp.float32) + scale_two * (
        scaled_two - unit_two * jnp.mean(scaled_two * unit_two, axis=-1, keepdims=True)
    )
    grad_attn = grad_hidden.astype(jnp.bfloat16)
    grad_hidden_local = lax.dynamic_slice_in_dim(grad_hidden, start, local_width, 1)
    grad_w_out = contract_rows(grouped, grad_attn)
    grad_grouped = contract_cols(grad_attn, w_out).reshape(rows_here, heads_here, HEAD_DIM)
    grad_group_gain = jnp.sum(grad_grouped * unit_heads, axis=0).reshape(local_width)
    scaled_heads = grad_grouped * gain_heads
    grad_heads = (
        group_scale
        * (scaled_heads - unit_heads * jnp.mean(scaled_heads * unit_heads, axis=-1, keepdims=True))
    ).astype(jnp.bfloat16)
    grad_split = grad_heads.reshape(seq_count, length, heads_here, HEAD_DIM)

    def backward_one(items):
        return attend_backward(
            items[0], items[1], items[2], items[3], items[4], items[5], kq_kernel, head_mix
        )

    grad_query, grad_keys, grad_values, kernel_terms, mix_terms = lax.map(
        backward_one,
        (split_heads[0], split_heads[1], split_heads[2], segments, grad_split, log_norms),
    )
    grad_proj = (
        jnp.stack([grad_query, grad_keys, grad_values])
        .astype(jnp.bfloat16)
        .reshape(3, rows_here, local_width)
    )
    grad_kernel = jnp.sum(kernel_terms, axis=0)
    grad_mix = jnp.sum(mix_terms, axis=0)
    grad_qkv = jnp.einsum("td,cte->cde", normed_one, grad_proj, preferred_element_type=jnp.float32)
    grad_one_part = jnp.einsum("cte,cde->td", grad_proj, w_qkv, preferred_element_type=jnp.float32)
    grad_one = lax.psum_scatter(
        grad_one_part.astype(jnp.bfloat16), "tensor", scatter_dimension=1, tiled=True
    ).astype(jnp.float32)
    unit_local = lax.dynamic_slice_in_dim(unit_one, start, local_width, 1)
    scaled_one = grad_one * attn_gain.astype(jnp.float32)
    row_total = lax.psum(jnp.sum(scaled_one * unit_local, axis=-1, keepdims=True), "tensor")
    tokens_grad = grad_hidden_local + scale_one * (
        scaled_one - unit_local * (row_total / full_width)
    )
    grad_gain_one = jnp.sum(grad_one * unit_local, axis=0)
    (
        grad_gain_one,
        grad_qkv,
        grad_kernel,
        grad_mix,
        grad_group_gain,
        grad_w_out,
        grad_gain_two,
        grad_gate_up,
        grad_down,
    ) = lax.psum(
        (
            grad_gain_one,
            grad_qkv,
            grad_kernel,
            grad_mix,
            grad_group_gain,
            grad_w_out,
            grad_gain_two,
            grad_gate_up,
            grad_down,
        ),
        "dp",
    )
    return (
        layer_out,
        tokens_grad,
        grad_gain_one,
        grad_qkv,
        grad_kernel,
        grad_mix,
        grad_group_gain,
        grad_w_out,
        grad_gain_two,
        grad_gate_up,
        grad_down,
    )


def solution(mesh):
    in_specs = (
        P("dp", "tensor"),
        P("dp", None),
        P("tensor"),
        P(None, None, "tensor"),
        P("tensor", None, None),
        P("tensor", None),
        P("tensor"),
        P("tensor", None),
        P("tensor"),
        P(None, None, "tensor"),
        P("tensor", None),
        P("dp", "tensor"),
    )
    out_specs = (
        P("dp", "tensor"),
        P("dp", "tensor"),
        P("tensor"),
        P(None, None, "tensor"),
        P("tensor", None, None),
        P("tensor", None),
        P("tensor"),
        P("tensor", None),
        P("tensor"),
        P(None, None, "tensor"),
        P("tensor", None),
    )
    return jax.shard_map(
        on_device, mesh=mesh, in_specs=in_specs, out_specs=out_specs, check_vma=False
    )
```

profile of v0, /device:TPU:0, one launch (start us, length us, event | category | flops | bytes accessed | tf_op | source)
XLA Modules:
  0.0 3078.3 jit_solution(3075463424177838024)
XLA Ops:
  29.7 11.2 all-gather.5.cloned.1.call-done
  50.7 8.6 multiply_select_fusion
  59.3 754.6 %fusion.168 = (f32[4,1024]{1,0:T(4,128)S(1)}, f32[4,1024,1024]{2,1,0:T(8,128)}) fusion(f32[4]{0:T(128)} %get-tuple-element.249, f32[4]{0:T(128)} %get-tuple-element.250, f32[4]{0:T(128)} %get-tuple-element.186, f32[4]{0:T(128)} %get-tuple-element.187, f32[4]{0:T(128)} %get-tuple-element.188, f32[4]{0:T(128)} %get-tuple-element.189, ...), kind=kLoop, calls=%fused_computation.489 | loop fusion | flops 557838336 | bytes 34620448 | tf_op jit(solution)/shard_map/while/body/eval_jaxpr/reduce_max | solution.py:106
  813.9 7.8 fusion.140
  862.4 111.2 %all-reduce.8.cloned.1.call-done = f32[1024,1536]{1,0:T(8,128)} async-done(((f32[1024,1536]{1,0:T(8,128)}), f32[1024,1536]{1,0:T(8,128)}) %all-reduce.8.cloned.1.call-update) | async-done | bytes 6291472 | tf_op jit(solution)/shard_map/psum | solution.py:192
  984.2 11.3 convolution_bitcast_fusion.3
  995.5 8.4 all-gather.7.cloned.1.call-done
  1003.9 11.5 fusion.147
  1017.4 10.5 convolution_bitcast_fusion.2
  1048.3 99.3 %all-reduce.10.cloned.1.call-done = f32[1024,1536]{1,0:T(8,128)} async-done(((f32[1024,1536]{1,0:T(8,128)}), f32[1024,1536]{1,0:T(8,128)}) %all-reduce.10.cloned.1.call-update) | async-done | bytes 6291472 | tf_op jit(solution)/shard_map/psum | solution.py:221
  1177.5 21.4 fusion.134
  1199.0 101.0 %multiply_reduce_fusion.54 = (f32[4]{0:T(128)}, f32[4]{0:T(128)}, f32[4]{0:T(128)}, f32[4]{0:T(128)}, f32[4]{0:T(128)}, /*index=5*/f32[4]{0:T(128)}, f32[4]{0:T(...) fusion(f32[4,1024,1024]{2,1,0:T(8,128)} %multiply_select_fusion, ...), kind=kOutput, calls=%fused_computation.329 | output fusion | flops 121639920 | bytes 83886304 | tf_op jit(solution)/shard_map/while/body/eval_jaxpr/sub | solution.py:123
  1300.0 771.0 %multiply_convert_fusion = bf16[4,1024,1024]{2,1,0:T(8,128)(2,1)} fusion(f32[4,1024,1024]{2,1,0:T(8,128)} %get-tuple-element.285, f32[4]{0:T(128)} %get-tuple-element.249, f32[4]{0:T(128)} %get-tuple-element.250, f32[4]{0:T(128)} %get-tuple-element.186, f32[4]{0:T(128)} %get-tuple-element.187, f32[4]{0:T(128)} %get-tuple-element.188, ...), kind=kLoop, calls=%fused_computation.341 | loop fusion | flops 562036736 | bytes 26215456 | tf_op jit(solution)/shard_map/while/body/eval_jaxpr/convert_element_type | solution.py:125
  2115.1 9.1 fusion.175
  2124.2 13.9 convolution_bitcast_fusion
  2148.6 25.6 copy.125
  2174.2 25.6 copy.126
  2211.7 181.0 %multiply_reduce_fusion.36 = (f32[4]{0:T(128)}, f32[4]{0:T(128)}, f32[4]{0:T(128)}, f32[4]{0:T(128)}, f32[4]{0:T(128)}, /*index=5*/f32[4]{0:T(128)}, f32[4]{0:T(...) fusion(f32[4,1024,1024]{2,1,0:T(8,128)} %get-tuple-element.285,, ...), kind=kLoop, calls=%fused_computation.311 | loop fusion | flops 150994912 | bytes 33554720 | tf_op jit(solution)/shard_map/while/body/eval_jaxpr/reduce_sum | solution.py:66
  2415.5 186.3 %multiply_reduce_fusion.18 = (f32[4]{0:T(128)}, f32[4]{0:T(128)}, f32[4]{0:T(128)}, f32[4]{0:T(128)}, f32[4]{0:T(128)}, /*index=5*/f32[4]{0:T(128)}, f32[4]{0:T(...) fusion(f32[4,1024,1024]{2,1,0:T(8,128)} %get-tuple-element.285,, ...), kind=kLoop, calls=%fused_computation.293 | loop fusion | flops 150994912 | bytes 33554720 | tf_op jit(solution)/shard_map/while/body/eval_jaxpr/reduce_sum | solution.py:66
  2604.4 174.2 %multiply_reduce_fusion = (f32[4]{0:T(128)}, f32[4]{0:T(128)}, f32[4]{0:T(128)}, f32[4]{0:T(128)}, f32[4]{0:T(128)}, /*index=5*/f32[4]{0:T(128)}, f32[4]{0:T(128...) fusion(f32[4,1024,1024]{2,1,0:T(8,128)} %get-tuple-element.285,, ...), kind=kLoop, calls=%fused_computation.275 | loop fusion | flops 150994912 | bytes 33554720 | tf_op jit(solution)/shard_map/while/body/eval_jaxpr/reduce_sum | solution.py:66
  2825.1 154.8 %fusion.174 = f32[2,2,2,1]{2,1,3,0:T(2,128)} fusion(f32[2,2,1024,1024]{2,1,3,0:T(2,128)} %copy.125, f32[2,2,1024,1024]{2,1,3,0:T(2,128)} %copy.126), kind=kOutput, calls=%fused_computation.495 | convolution fusion | flops 100663296 | bytes 33554464 | tf_op jit(solution)/shard_map/while/body/eval_jaxpr/grqk,gsqk->grs/dot_general | solution.py:91
  2992.5 38.2 %all-reduce.2 = (f32[384]{0:T(512)}, f32[4,6,11]{2,1,0:T(8,128)}, f32[4,2]{0,1:T(2,128)}, f32[384]{0:T(512)}, f32[384]{0:T(512)}) all-reduce(f32[384]{0:T(512)} %get-tuple-element.181, f32[4,6,11]{2,1,0:T(8,128)S(1)} %reduce_sum.848, f32[4,2]{0,1:T(2,128)} %copy.136, f32[384]{0:T(512)} %reshape.232, ...), channel_id=1, replica_groups=mesh['dp'=8,'tensor'=4] {'dp'}, use_global_device_ids=true, to_apply=%region_15.16 | all-reduce | flops 1424 | bytes 11392 | tf_op jit(solution)/shard_map/psum | solution.py:279
  3041.4 8.0 copy.129
  3049.4 12.6 copy.131
  (266 shorter events, 306.2 us)
Async XLA Ops:
  7.2 36.3 %copy-start = (bf16[3,1536,384]{2,1,0:T(8,128)(2,1)S(1)}, bf16[3,1536,384]{2,1,0:T(8,128)(2,1)}, u32[]{:S(2)}) copy-start(bf16[3,1536,384]{2,1,0:T(8,128)(2,1)} %param.15) | copy-start | bytes 10616836
  7.2 33.6 %all-gather.5.cloned.1.call-start = ((), (), s32[]{:S(2)}) async-start(), calls=%async_computation.2 | async-start | bytes 3932160 | tf_op jit(solution)/shard_map/all_gather | solution.py:165
  7.9 965.7 %all-reduce.8.cloned.1.call-start = ((), (), s32[]{:S(2)}) async-start(), calls=%async_computation.3 | async-start | bytes 12582912 | tf_op jit(solution)/shard_map/psum | solution.py:192
  11.0 39.6 %copy-start.35 = (f32[2,2,2]{1,0,2:T(2,128)}, f32[2,2,2]{1,0,2:T(2,128)S(1)}, u32[]{:S(2)}) copy-start(f32[2,2,2]{1,0,2:T(2,128)S(1)} %reshape.226) | copy-start | bytes 100
  43.5 15.8 copy-start.31
  853.9 150.0 %all-gather.7.cloned.1.call-start = ((), (), s32[]{:S(2)}) async-start(), calls=%async_computation.4 | async-start | bytes 3932160 | tf_op jit(solution)/shard_map/all_gather | solution.py:209
  854.6 293.0 %all-reduce.10.cloned.1.call-start = ((), (), s32[]{:S(2)}) async-start(), calls=%async_computation.5 | async-start | bytes 12582912 | tf_op jit(solution)/shard_map/psum | solution.py:221
  1027.9 1954.7 %reduce-scatter.7.cloned.1.call-start = ((), (), s32[]{:S(2)}) async-start(), calls=%async_computation.6 | async-start | bytes 3932160
  1035.9 111.7 %copy-start.27 = (f32[1536]{0:T(1024)S(1)}, f32[1536]{0:T(1024)}, u32[]{:S(2)}) copy-start(f32[1536]{0:T(1024)} %reshape.239) | copy-start | bytes 18436
  1035.9 111.7 %copy-start.30 = (f32[1024]{0:T(1024)S(1)}, f32[1024]{0:T(1024)}, u32[]{:S(2)}) copy-start(f32[1024]{0:T(1024)} %copy-done.29) | copy-start | bytes 12292
  1048.2 1939.4 %reduce-scatter.9.cloned.1.call-start = ((), (), s32[]{:S(2)}) async-start(), calls=%async_computation.7 | async-start | bytes 3932160
  1199.0 101.0 %copy-start.38 = (f32[4]{0:T(128)S(1)}, f32[4]{0:T(128)}, u32[]{:S(2)}) copy-start(f32[4]{0:T(128)} %get-tuple-element.204) | copy-start | bytes 52
  2115.0 926.4 %all-reduce.12.cloned.1.call-start = ((), (), s32[]{:S(2)}) async-start(), calls=%async_computation.8 | async-start | bytes 56623104 | tf_op jit(solution)/shard_map/psum | solution.py:279
  2115.1 23.1 slice-start
  2124.2 16.8 copy-start.9
  2124.2 16.8 copy-start.20
  2124.2 16.8 copy-start.21
  2124.2 16.8 copy-start.22
  2124.2 16.8 copy-start.32
  2124.2 16.8 copy-start.37
  2174.2 25.6 copy-start.36
  2174.2 26.2 copy-start.48
  2174.2 26.3 copy-start.47
  2174.2 26.4 copy-start.46
  (36 other events, 259.8 us)
Sparse Core Ops, SparseCore 0:
  9.6 31.1 all-gather.4
  854.0 119.5 all-reduce.7
  975.2 28.6 all-gather.6
  1028.0 119.5 all-reduce.9
  1150.0 38.1 reduce-scatter.6
  2115.1 37.7 reduce-scatter.8
  2159.0 836.7 all-reduce.11
where the time goes:
time: 3090 us; the launch traced here: 3080 us
  other arithmetic  2250 us (73%)
  matrix products  276 us (9%)
  local copies, waits for them, and re-layouts  249 us (8%)
  waiting for transfers between devices  232 us (8%)
  blocking collectives  55.1 us (2%)
    convert_element_type x1, other arithmetic, attend_backward(): (jnp.where(valid, grad_masked, 0.0) * scale).astype(jnp.bfloat16)  771 us
    reduce_max x1, other arithmetic, attend_forward(): peak = jnp.max(logits, axis=-1, keepdims=True)  755 us
    reduce_sum x3, other arithmetic, conv_back(): kernel_terms.append(jnp.sum(grad_logits * window_in, axis=(1, 2)))  541 us
    dot_general x1, matrix products, mix_back(): grad_mix = jnp.einsum('grqk,gsqk->grs', paired_grad, paired, precision=HIGH)  155 us
    psum x1, waiting for transfers between devices, on_device(): attn = lax.psum(attn_part, 'tensor')  111 us
    sub x1, other arithmetic, attend_backward(): grad_probs - jnp.sum(grad_probs * probs, axis=-1, keepdims=True)  101 us
    psum x1, waiting for transfers between devices, on_device(): grad_two = lax.psum(grad_two_part, 'tensor')  99.3 us
    another operation x67, local copies, waits for them, and re-layouts, conv_back(): jnp.stack(kernel_terms, axis=1).reshape(heads_here, query_taps, key_taps)  82.4 us
  transfers between devices with their start and end apart: 7, of which 4 were waited for; matrix products, arithmetic and copies ran while one was open for 62% of the time, Pallas kernels for 0%

commit v1 on v0

--- a/solution.py
+++ b/solution.py
@@ -218,7 +218,7 @@
     grad_two_part = jnp.einsum(
         "ctf,cdf->td", grad_pair, w_gate_up, preferred_element_type=jnp.float32
     )
-    grad_two = lax.psum(grad_two_part, "tensor")
+    grad_two = jnp.sum(lax.all_gather(grad_two_part, "tensor"), axis=0)
     grad_gain_two = lax.dynamic_slice_in_dim(
         jnp.sum(grad_two * unit_two, axis=0), start, local_width, 0
     )

time: 3090 us -> 3180 us (1.029)
  other arithmetic: 2250 us -> 2310 us
  waiting for transfers between devices: 232 us -> 265 us
    all_gather x0 -> x1, waiting for transfers between devices: none -> 132 us  [on_device(): grad_two = jnp.sum(lax.all_gather(grad_two_part, 'tensor'), axis=0)]
    psum x1 -> x0, waiting for transfers between devices: 99.3 us -> none  [on_device(): grad_two = lax.psum(grad_two_part, 'tensor')]
    convert_element_type x1, other arithmetic: 771 us -> 804 us  [attend_backward(): (jnp.where(valid, grad_masked, 0.0) * scale).astype(jnp.bfloat16)]
  transfers between devices with their start and end apart: 7 -> 7, of which waited for: 4 -> 4; matrix products, arithmetic and copies ran while one was open for 62% -> 61% of each run, Pallas kernels for 0% -> 0%
where the time goes in v1:
time: 3180 us; the launch traced here: 3170 us
  other arithmetic  2310 us (73%)
  matrix products  278 us (9%)
  waiting for transfers between devices  265 us (8%)
  local copies, waits for them, and re-layouts  250 us (8%)
  blocking collectives  55.5 us (2%)
    convert_element_type x1, other arithmetic, attend_backward(): (jnp.where(valid, grad_masked, 0.0) * scale).astype(jnp.bfloat16)  804 us
    reduce_max x1, other arithmetic, attend_forward(): peak = jnp.max(logits, axis=-1, keepdims=True)  778 us
    reduce_sum x3, other arithmetic, conv_back(): kernel_terms.append(jnp.sum(grad_logits * window_in, axis=(1, 2)))  533 us
    dot_general x1, matrix products, mix_back(): grad_mix = jnp.einsum('grqk,gsqk->grs', paired_grad, paired, precision=HIGH)  155 us
    all_gather x1, waiting for transfers between devices, on_device(): grad_two = jnp.sum(lax.all_gather(grad_two_part, 'tensor'), axis=0)  132 us
    psum x1, waiting for transfers between devices, on_device(): attn = lax.psum(attn_part, 'tensor')  111 us
    sub x1, other arithmetic, attend_backward(): grad_probs - jnp.sum(grad_probs * probs, axis=-1, keepdims=True)  99.6 us
    another operation x67, local copies, waits for them, and re-layouts, conv_back(): jnp.stack(kernel_terms, axis=1).reshape(heads_here, query_taps, key_taps)  82.8 us
  transfers between devices with their start and end apart: 7, of which 4 were waited for; matrix products, arithmetic and copies ran while one was open for 61% of the time, Pallas kernels for 0%

profile of v1, /device:TPU:0, one launch (start us, length us, event | category | flops | bytes accessed | tf_op | source)
XLA Modules:
  0.0 3173.7 jit_solution(16991417739232420487)
XLA Ops:
  29.6 11.2 all-gather.7.cloned.1.call-done
  50.7 8.7 multiply_select_fusion
  59.4 777.6 %fusion.168 = (f32[4,1024]{1,0:T(4,128)S(1)}, f32[4,1024,1024]{2,1,0:T(8,128)}) fusion(f32[4]{0:T(128)} %get-tuple-element.249, f32[4]{0:T(128)} %get-tuple-element.250, f32[4]{0:T(128)} %get-tuple-element.186, f32[4]{0:T(128)} %get-tuple-element.187, f32[4]{0:T(128)} %get-tuple-element.188, f32[4]{0:T(128)} %get-tuple-element.189, ...), kind=kLoop, calls=%fused_computation.489 | loop fusion | flops 557838336 | bytes 34620448 | tf_op jit(solution)/shard_map/while/body/eval_jaxpr/reduce_max | solution.py:106
  885.6 111.2 %all-reduce.7.cloned.1.call-done = f32[1024,1536]{1,0:T(8,128)} async-done(((f32[1024,1536]{1,0:T(8,128)}), f32[1024,1536]{1,0:T(8,128)}) %all-reduce.7.cloned.1.call-update) | async-done | bytes 6291472 | tf_op jit(solution)/shard_map/psum | solution.py:192
  1007.3 11.3 convolution_bitcast_fusion.3
  1018.7 8.4 all-gather.9.cloned.1.call-done
  1027.1 11.5 fusion.147
  1040.6 10.5 convolution_bitcast_fusion.2
  1059.1 9.4 convolution_convert_fusion
  1073.8 132.4 %all-gather.11.cloned.1.call-done = f32[4096,1536]{1,0:T(8,128)} async-done(((f32[1024,1536]{1,0:T(8,128)}), f32[4096,1536]{1,0:T(8,128)}) %all-gather.11.cloned.1.call-update) | async-done | bytes 25165840 | tf_op jit(solution)/shard_map/all_gather | solution.py:221
  1206.1 13.9 reduce_sum.786
  1248.7 21.5 fusion.134
  1270.1 99.6 %multiply_reduce_fusion.54 = (f32[4]{0:T(128)}, f32[4]{0:T(128)}, f32[4]{0:T(128)}, f32[4]{0:T(128)}, f32[4]{0:T(128)}, /*index=5*/f32[4]{0:T(128)}, f32[4]{0:T(...) fusion(f32[4,1024,1024]{2,1,0:T(8,128)} %multiply_select_fusion, ...), kind=kOutput, calls=%fused_computation.329 | output fusion | flops 121639920 | bytes 83886304 | tf_op jit(solution)/shard_map/while/body/eval_jaxpr/sub | solution.py:123
  1369.8 804.2 %multiply_convert_fusion = bf16[4,1024,1024]{2,1,0:T(8,128)(2,1)} fusion(f32[4,1024,1024]{2,1,0:T(8,128)} %get-tuple-element.285, f32[4]{0:T(128)} %get-tuple-element.249, f32[4]{0:T(128)} %get-tuple-element.250, f32[4]{0:T(128)} %get-tuple-element.186, f32[4]{0:T(128)} %get-tuple-element.187, f32[4]{0:T(128)} %get-tuple-element.188, ...), kind=kLoop, calls=%fused_computation.341 | loop fusion | flops 562036736 | bytes 26215456 | tf_op jit(solution)/shard_map/while/body/eval_jaxpr/convert_element_type | solution.py:125
  2218.1 9.0 fusion.175
  2227.1 14.1 convolution_bitcast_fusion
  2256.6 25.5 copy.125
  2282.2 25.5 copy.126
  2321.1 178.4 %multiply_reduce_fusion.36 = (f32[4]{0:T(128)}, f32[4]{0:T(128)}, f32[4]{0:T(128)}, f32[4]{0:T(128)}, f32[4]{0:T(128)}, /*index=5*/f32[4]{0:T(128)}, f32[4]{0:T(...) fusion(f32[4,1024,1024]{2,1,0:T(8,128)} %get-tuple-element.285,, ...), kind=kLoop, calls=%fused_computation.311 | loop fusion | flops 150994912 | bytes 33554720 | tf_op jit(solution)/shard_map/while/body/eval_jaxpr/reduce_sum | solution.py:66
  2522.9 183.7 %multiply_reduce_fusion.18 = (f32[4]{0:T(128)}, f32[4]{0:T(128)}, f32[4]{0:T(128)}, f32[4]{0:T(128)}, f32[4]{0:T(128)}, /*index=5*/f32[4]{0:T(128)}, f32[4]{0:T(...) fusion(f32[4,1024,1024]{2,1,0:T(8,128)} %get-tuple-element.285,, ...), kind=kLoop, calls=%fused_computation.293 | loop fusion | flops 150994912 | bytes 33554720 | tf_op jit(solution)/shard_map/while/body/eval_jaxpr/reduce_sum | solution.py:66
  2709.1 171.1 %multiply_reduce_fusion = (f32[4]{0:T(128)}, f32[4]{0:T(128)}, f32[4]{0:T(128)}, f32[4]{0:T(128)}, f32[4]{0:T(128)}, /*index=5*/f32[4]{0:T(128)}, f32[4]{0:T(128...) fusion(f32[4,1024,1024]{2,1,0:T(8,128)} %get-tuple-element.285,, ...), kind=kLoop, calls=%fused_computation.275 | loop fusion | flops 150994912 | bytes 33554720 | tf_op jit(solution)/shard_map/while/body/eval_jaxpr/reduce_sum | solution.py:66
  2926.5 154.8 %fusion.174 = f32[2,2,2,1]{2,1,3,0:T(2,128)} fusion(f32[2,2,1024,1024]{2,1,3,0:T(2,128)} %copy.125, f32[2,2,1024,1024]{2,1,3,0:T(2,128)} %copy.126), kind=kOutput, calls=%fused_computation.495 | convolution fusion | flops 100663296 | bytes 33554464 | tf_op jit(solution)/shard_map/while/body/eval_jaxpr/grqk,gsqk->grs/dot_general | solution.py:91
  3087.6 38.5 %all-reduce.2 = (f32[384]{0:T(512)}, f32[4,6,11]{2,1,0:T(8,128)}, f32[4,2]{0,1:T(2,128)}, f32[384]{0:T(512)}, f32[384]{0:T(512)}) all-reduce(f32[384]{0:T(512)} %get-tuple-element.181, f32[4,6,11]{2,1,0:T(8,128)S(1)} %reduce_sum.858, f32[4,2]{0,1:T(2,128)} %copy.136, f32[384]{0:T(512)} %reshape.232, ...), channel_id=1, replica_groups=mesh['dp'=8,'tensor'=4] {'dp'}, use_global_device_ids=true, to_apply=%region_15.16 | all-reduce | flops 1424 | bytes 11392 | tf_op jit(solution)/shard_map/psum | solution.py:279
  3144.9 12.6 copy.131
  (267 shorter events, 314.1 us)
Async XLA Ops:
  7.2 36.3 %copy-start = (bf16[3,1536,384]{2,1,0:T(8,128)(2,1)S(1)}, bf16[3,1536,384]{2,1,0:T(8,128)(2,1)}, u32[]{:S(2)}) copy-start(bf16[3,1536,384]{2,1,0:T(8,128)(2,1)} %param.15) | copy-start | bytes 10616836
  7.2 33.6 %all-gather.7.cloned.1.call-start = ((), (), s32[]{:S(2)}) async-start(), calls=%async_computation.2 | async-start | bytes 3932160 | tf_op jit(solution)/shard_map/all_gather | solution.py:165
  7.9 988.9 %all-reduce.7.cloned.1.call-start = ((), (), s32[]{:S(2)}) async-start(), calls=%async_computation.3 | async-start | bytes 12582912 | tf_op jit(solution)/shard_map/psum | solution.py:192
  11.0 39.6 %copy-start.35 = (f32[2,2,2]{1,0,2:T(2,128)}, f32[2,2,2]{1,0,2:T(2,128)S(1)}, u32[]{:S(2)}) copy-start(f32[2,2,2]{1,0,2:T(2,128)S(1)} %reshape.226) | copy-start | bytes 100
  43.5 15.9 copy-start.31
  877.1 150.0 %all-gather.9.cloned.1.call-start = ((), (), s32[]{:S(2)}) async-start(), calls=%async_computation.4 | async-start | bytes 3932160 | tf_op jit(solution)/shard_map/all_gather | solution.py:209
  877.8 328.3 %all-gather.11.cloned.1.call-start = ((), (), s32[]{:S(2)}) async-start(), calls=%async_computation.5 | async-start | bytes 31457280 | tf_op jit(solution)/shard_map/all_gather | solution.py:221
  1051.1 1200.5 %reduce-scatter.7.cloned.1.call-start = ((), (), s32[]{:S(2)}) async-start(), calls=%async_computation.6 | async-start | bytes 3932160
  1073.7 146.3 %copy-start.27 = (f32[1536]{0:T(1024)S(1)}, f32[1536]{0:T(1024)}, u32[]{:S(2)}) copy-start(f32[1536]{0:T(1024)} %reshape.240) | copy-start | bytes 18436
  1073.7 146.3 %copy-start.30 = (f32[1024]{0:T(1024)S(1)}, f32[1024]{0:T(1024)}, u32[]{:S(2)}) copy-start(f32[1024]{0:T(1024)} %copy-done.29) | copy-start | bytes 12292
  1073.7 2009.0 %reduce-scatter.9.cloned.1.call-start = ((), (), s32[]{:S(2)}) async-start(), calls=%async_computation.7 | async-start | bytes 3932160
  1270.1 99.6 %copy-start.38 = (f32[4]{0:T(128)S(1)}, f32[4]{0:T(128)}, u32[]{:S(2)}) copy-start(f32[4]{0:T(128)} %get-tuple-element.204) | copy-start | bytes 52
  2218.0 918.8 %all-reduce.9.cloned.1.call-start = ((), (), s32[]{:S(2)}) async-start(), calls=%async_computation.8 | async-start | bytes 56623104 | tf_op jit(solution)/shard_map/psum | solution.py:279
  2218.1 23.1 slice-start
  2227.1 16.9 copy-start.9
  2227.1 16.9 copy-start.20
  2227.1 16.9 copy-start.21
  2227.1 16.9 copy-start.22
  2227.1 16.9 copy-start.32
  2227.1 16.9 copy-start.37
  2282.2 26.8 copy-start.36
  2282.2 27.5 copy-start.48
  2282.2 27.6 copy-start.47
  2282.2 27.7 copy-start.46
  (36 other events, 254.2 us)
Sparse Core Ops, SparseCore 0:
  9.6 31.1 all-gather.6
  877.2 119.5 all-reduce.6
  998.4 28.6 all-gather.8
  1051.2 154.8 all-gather.10
  1208.5 37.9 reduce-scatter.6
  2218.1 38.4 reduce-scatter.8
  2262.6 836.8 all-reduce.8
